TPU v7x, 32 devices: a whole 2x2x4 slice. The times are simulated.
32 devices in a mesh: bead: 16 (over z, y, x), space: 2 (over core).
Axes of the slice: x: 2, y: 2, z: 4, core: 2. Of those that a mesh axis runs over, the one named last changes fastest.
Arguments:
- positions: float32 [32, 3, 16384], P('bead', None, 'space'), may hold values from -6 to 6
- momenta: float32 [32, 3, 16384], P('bead', None, 'space'), may hold values from -6 to 6
- forces: float32 [32, 3, 16384], P('bead', None, 'space'), may hold values from -6 to 6
- gle_drift: float32 [32, 5, 5], replicated, may hold values from -0.25 to 0.98, as said below
- gle_noise_mix: float32 [32, 5, 5], replicated, may hold values from -1.5 to 1.5
- aux_momenta: float32 [32, 4, 3, 16384], P(None, None, None, ('space', 'bead')), may hold values from -6 to 6
- noise: float32 [2, 32, 5, 3, 16384], P(None, None, None, None, ('space', 'bead')), may hold values from -6 to 6
Outputs:
- positions_out: float32 [32, 3, 16384], P('bead', None, 'space')
- momenta_out: float32 [32, 3, 16384], P('bead', None, 'space')
- forces_out: float32 [32, 3, 16384], P('bead', None, 'space')
- aux_out: float32 [32, 4, 3, 16384], P(None, None, None, ('space', 'bead'))
Inputs may be any that keep to these rules, and one draw needn't show every extreme that they name: `gle_drift`: one matrix a mode; diagonal entries positive.
All inputs are finite; a program needn't handle non-finite values.
Results may differ from a plain program's by a relative error of at most 0.00012.
Values sent between devices are 32-bit elements; how exact they have to be, the bound alone decides.
No kernel may reach another device: no remote copies, remote signals or barrier semaphores. Data moves between devices by JAX's collectives and lax.ppermute only.
A program may use at most 64 MiB of HBM per device.

v0:
```python
import math
import jax
import jax.numpy as jnp
from jax import lax
from jax.sharding import PartitionSpec as P

BEADS = 32
CELL_ATOMS = 128
STEPS = 2
time_step = 0.5
cycle_freq = 1.5
cell_length = 2.0
pair_strength = 0.1
pair_range = 1.0


def passed_along(block, axis, distance):
    devices = range(lax.axis_size(axis))
    route = [((i - distance) % len(devices), i) for i in devices]
    return lax.ppermute(block, axis, route)


def mode_basis():
    index = jnp.arange(BEADS)
    bead_pos = index.astype(jnp.float32)[:, None]
    mode_pos = index.astype(jnp.float32)[None, :]
    phase = 2.0 * jnp.pi * bead_pos * mode_pos / BEADS
    kk = index[None, :]
    low = jnp.sqrt(1.0 / BEADS) + 0.0 * phase
    basis = jnp.where(
        kk == 0,
        low,
        jnp.where(
            kk < BEADS // 2,
            jnp.sqrt(2.0 / BEADS) * jnp.cos(phase),
            jnp.where(
                kk == BEADS // 2,
                jnp.sqrt(1.0 / BEADS) * jnp.cos(phase),
                jnp.sqrt(2.0 / BEADS) * jnp.sin(phase),
            ),
        ),
    )
    freq = 2.0 * cycle_freq * jnp.sin(jnp.pi * index.astype(jnp.float32) / BEADS)
    return (basis, freq, index)


def tile_weight(center, other):
    sa = jnp.sum(center * center, axis=1)
    sb = jnp.sum(other * other, axis=1)
    cross = jnp.einsum("xcni,xcnj->xnij", center, other, precision=lax.Precision.HIGHEST)
    dist = sa[:, :, :, None] + sb[:, :, None, :] - 2.0 * cross
    return jnp.exp(-dist / (2.0 * pair_range))


def pull(center, other):
    weight = tile_weight(center, other)
    rowsum = jnp.sum(weight, axis=3)
    pulled = jnp.einsum("xnij,xcnj->xcni", weight, other, precision=lax.Precision.HIGHEST)
    return pair_strength / pair_range * (center * rowsum[:, None] - pulled)


def mutual(center, other):
    weight = tile_weight(center, other)
    rowsum = jnp.sum(weight, axis=3)
    colsum = jnp.sum(weight, axis=2)
    pulled = jnp.einsum("xnij,xcnj->xcni", weight, other, precision=lax.Precision.HIGHEST)
    pushed = jnp.einsum("xnij,xcni->xcnj", weight, center, precision=lax.Precision.HIGHEST)
    coef = pair_strength / pair_range
    return (coef * (center * rowsum[:, None] - pulled), coef * (other * colsum[:, None] - pushed))


def moved(cells, delta):
    offset = jnp.asarray([delta * cell_length, 0.0, 0.0], dtype=cells.dtype).reshape(1, 3, 1, 1)
    return cells + offset


def pair_forces(positions):
    beads_here = positions.shape[0]
    cells = positions.shape[2] // CELL_ATOMS
    block = math.gcd(cells, 16)
    following = passed_along(positions[:, :, :CELL_ATOMS], "space", -1)
    grid = jnp.concatenate([positions, following], axis=2).reshape(
        beads_here, 3, cells + 1, CELL_ATOMS
    )

    def accumulate_pairs(number, total):
        start = number * block
        center = lax.dynamic_slice_in_dim(grid, start, block, 2)
        other = lax.dynamic_slice_in_dim(grid, start + 1, block, 2)
        own = pull(center, center)
        on_center, on_other = mutual(center, moved(other, 1))
        total = lax.dynamic_update_slice_in_dim(
            total, lax.dynamic_slice_in_dim(total, start, block, 2) + own + on_center, start, 2
        )
        return lax.dynamic_update_slice_in_dim(
            total, lax.dynamic_slice_in_dim(total, start + 1, block, 2) + on_other, start + 1, 2
        )

    total = jnp.zeros((beads_here, 3, cells + 1, CELL_ATOMS), positions.dtype)
    total = lax.fori_loop(0, cells // block, accumulate_pairs, total)
    returned = passed_along(total[:, :, cells], "space", 1)
    first = total[:, :, 0] + returned
    result = jnp.concatenate([first[:, :, None], total[:, :, 1:cells]], axis=2)
    return result.reshape(positions.shape)


def mode_step(qbeads, pbeads, aux, noise_now, basis, cosine, sinc, wsin, gle_drift, gle_noise_mix):
    qmode = jnp.einsum("jk,jcn->kcn", basis, qbeads, precision=lax.Precision.HIGHEST)
    pmode = jnp.einsum("jk,jcn->kcn", basis, pbeads, precision=lax.Precision.HIGHEST)
    state = jnp.concatenate([pmode[:, None], aux], axis=1)
    state = jnp.einsum(
        "kab,kbcn->kacn", gle_drift, state, precision=lax.Precision.HIGHEST
    ) + jnp.einsum("kab,kbcn->kacn", gle_noise_mix, noise_now, precision=lax.Precision.HIGHEST)
    pmode = state[:, 0]
    qnext = qmode * cosine + sinc * pmode
    pmode = pmode * cosine - wsin * qmode
    qbeads = jnp.einsum("jk,kcn->jcn", basis, qnext, precision=lax.Precision.HIGHEST)
    pbeads = jnp.einsum("jk,kcn->jcn", basis, pmode, precision=lax.Precision.HIGHEST)
    return (qbeads, pbeads, state[:, 1:])


def on_device(positions, momenta, forces, gle_drift, gle_noise_mix, aux_momenta, noise):
    beads_here = positions.shape[0]
    atoms_here = positions.shape[2]
    groups = lax.axis_size("bead")
    share = atoms_here // (2 * groups)
    basis, freq, index = mode_basis()
    cosine = jnp.cos(time_step * freq)[:, None, None]
    safe = jnp.where(index == 0, 1.0, freq)
    sinc = jnp.where(index == 0, time_step, jnp.sin(time_step * freq) / safe)[:, None, None]
    wsin = (freq * jnp.sin(time_step * freq))[:, None, None]
    half = 0.5 * time_step
    aux = aux_momenta
    force = forces
    for step in range(STEPS):
        momenta = momenta + half * force
        shaped_q = positions.reshape(beads_here, 3, 2, groups * share)
        shaped_p = momenta.reshape(beads_here, 3, 2, groups * share)
        owned_q, owned_p = (
            lax.all_to_all(shaped_q, "bead", split_axis=3, concat_axis=0, tiled=True),
            lax.all_to_all(shaped_p, "bead", split_axis=3, concat_axis=0, tiled=True),
        )
        new_q, new_p, aux = mode_step(
            owned_q.reshape(BEADS, 3, 2 * share),
            owned_p.reshape(BEADS, 3, 2 * share),
            aux,
            noise[step],
            basis,
            cosine,
            sinc,
            wsin,
            gle_drift,
            gle_noise_mix,
        )
        back_q, back_p = (
            lax.all_to_all(
                new_q.reshape(BEADS, 3, 2, share), "bead", split_axis=0, concat_axis=3, tiled=True
            ),
            lax.all_to_all(
                new_p.reshape(BEADS, 3, 2, share), "bead", split_axis=0, concat_axis=3, tiled=True
            ),
        )
        positions = back_q.reshape(beads_here, 3, atoms_here)
        momenta = back_p.reshape(beads_here, 3, atoms_here)
        force = pair_forces(positions)
        momenta = momenta + half * force
    return (positions, momenta, force, aux)


def solution(mesh):
    in_specs = (
        P("bead", None, "space"),
        P("bead", None, "space"),
        P("bead", None, "space"),
        P(),
        P(),
        P(None, None, None, ("space", "bead")),
        P(None, None, None, None, ("space", "bead")),
    )
    out_specs = (
        P("bead", None, "space"),
        P("bead", None, "space"),
        P("bead", None, "space"),
        P(None, None, None, ("space", "bead")),
    )
    return jax.shard_map(
        on_device, mesh=mesh, in_specs=in_specs, out_specs=out_specs, check_vma=False
    )
```

profile of v0, /device:TPU:1, one launch (start us, length us, event | category | flops | bytes accessed | tf_op | source)
XLA Modules:
  0.0 409.7 jit_solution(560465266027311314)
XLA Ops:
  2.0 8.3 %copy.360 = f32[2,3,2,4096]{1,2,0,3:T(2,128)} copy(f32[2,3,2,4096]{3,2,0,1:T(2,128)S(1)} %reshape.141) | data formatting | bytes 393216 | tf_op jit(solution)/shard_map/reshape | solution.py:138
  10.3 14.3 %reshape.167 = f32[16,1,3072]{2,1,0:T(1,128)} reshape(f32[4096,2,2,3]{3,2,1,0:T(2,128)} %bitcast.238) | data formatting | bytes 393216
  24.6 7.4 %all-to-all-start.1 = ((f32[16,1,3072]{2,1,0:T(1,128)}), f32[16,1,3072]{2,1,0:T(1,128)S(1)}, u32[]{:S(2)}, u32[]{:S(2)}) async-start(f32[16,1,3072]{2,1,0:T(1,128)} %reshape.167), calls=%async_computation.1 | async-start | bytes 393216 | tf_op jit(solution)/shard_map/all_to_all | solution.py:141
  32.7 8.3 %copy.356 = f32[2,3,2,4096]{1,2,0,3:T(2,128)} copy(f32[2,3,2,4096]{3,2,0,1:T(2,128)S(1)} %reshape.139) | data formatting | bytes 393216 | tf_op jit(solution)/shard_map/reshape | solution.py:137
  41.0 14.2 %reshape.165 = f32[16,1,3072]{2,1,0:T(1,128)} reshape(f32[4096,2,2,3]{3,2,1,0:T(2,128)} %bitcast.239) | data formatting | bytes 393216
  57.0 6.5 %all-to-all-start = ((f32[16,1,3072]{2,1,0:T(1,128)}), f32[16,1,3072]{2,1,0:T(1,128)S(1)}, u32[]{:S(2)}, u32[]{:S(2)}) async-start(f32[16,1,3072]{2,1,0:T(1,128)} %reshape.165), calls=%async_computation | async-start | bytes 393216 | tf_op jit(solution)/shard_map/all_to_all | solution.py:140
  68.3 14.8 %reshape.168 = f32[4096,2,2,3]{3,2,1,0:T(2,128)} reshape(f32[16,3072]{1,0:T(8,128)S(1)} %reduce.1) | data formatting | bytes 393216
  83.1 6.8 %copy.423 = f32[2,3,2,16,256]{4,3,2,1,0:T(8,128)S(1)} copy(f32[2,3,2,16,256]{1,2,0,4,3:T(2,128)} %bitcast.240) | data formatting | bytes 393216 | tf_op jit(solution)/shard_map/all_to_all | solution.py:141
  92.1 14.8 %reshape.166 = f32[4096,2,2,3]{3,2,1,0:T(2,128)} reshape(f32[16,3072]{1,0:T(8,128)S(1)} %reduce) | data formatting | bytes 393216
  107.0 7.0 %copy.421 = f32[2,3,2,16,256]{4,3,2,1,0:T(8,128)S(1)} copy(f32[2,3,2,16,256]{1,2,0,4,3:T(2,128)} %bitcast.241) | data formatting | bytes 393216 | tf_op jit(solution)/shard_map/all_to_all | solution.py:140
  121.2 6.4 %all-to-all-start.2 = ((f32[32,3,2,256]{3,2,1,0:T(2,128)}), f32[32,3,2,256]{3,2,1,0:T(2,128)S(1)}, u32[]{:S(2)}, u32[]{:S(2)}) async-start(f32[32,3,2,256]{3,2,1,0:T(2,128)} %copy.370), calls=%async_computation.2 | async-start | bytes 393216 | tf_op jit(solution)/shard_map/all_to_all | solution.py:156
  127.7 7.0 %all-to-all-done.2 = f32[32,3,2,256]{3,2,1,0:T(2,128)S(1)} async-done(((f32[32,3,2,256]{3,2,1,0:T(2,128)}), f32[32,3,2,256]{3,2,1,0:T(2,128)S(1)}, u32[]{:S(2)}, u32[]{:S(2)}) %all-to-all-start.2) | async-done | bytes 196640 | tf_op jit(solution)/shard_map/all_to_all | solution.py:156
  143.3 64.1 %while.32 = (s32[]{:T(128)}, f32[2,3,65,128]{3,1,2,0:T(4,128)S(1)}, f32[2,3,65,128]{3,1,2,0:T(4,128)S(1)}, s32[]{:T(128)}, s32[]{:T(128)}, /*index=5*/s32[]{:T(128)}, s32[]{:T(128)}, s32[]{:T(128)}, f32[3]{0:T(128)S(1)}) while((s32[]{:T(128)}, f32[2,3,65,128]{3,1,2,0:T(4,128)S(1)}, f32[2,3,65,128]{3,1,2,0:T(4,128)S(1)}, ...), condition=%wide.region_6.7_spmd.clone, body=%wide.region_0.6_spmd.sunk.clone.sunk | while | flops 101412872 | bytes 11750121 | solution.py:100
  144.0 4.5 %fusion.237 = (f32[2,16,128]{2,1,0:T(8,128)S(1)}, f32[2,16,128]{2,1,0:T(8,128)S(1)}, f32[2,16,128,128]{2,3,1,0:T(8,128)S(1)}) fusion(f32[2,3,65,128]{3,1,2,0:T(4,128)S(1)} %get-tuple-element.447, s32[]{:T(128)S(6)} %select_n.174, f32[3]{0:T(128)S(1)} %get-tuple-element.453, s32[]{:T(128)S(6)} %select_n.173, ...), kind=kOutput, calls=%fused_computation.231.clone.1 | convolution fusion | flops 22548480 | bytes 2294280 | tf_op jit(solution)/shard_map/while/body/eval_jaxpr/xcni,xcnj->xnij/dot_general | solution.py:50
  159.8 4.5 %fusion.237 = (f32[2,16,128]{2,1,0:T(8,128)S(1)}, f32[2,16,128]{2,1,0:T(8,128)S(1)}, f32[2,16,128,128]{2,3,1,0:T(8,128)S(1)}) fusion(f32[2,3,65,128]{3,1,2,0:T(4,128)S(1)} %get-tuple-element.447, s32[]{:T(128)S(6)} %select_n.174, f32[3]{0:T(128)S(1)} %get-tuple-element.453, s32[]{:T(128)S(6)} %select_n.173, ...), kind=kOutput, calls=%fused_computation.231.clone.1 | convolution fusion | flops 22548480 | bytes 2294280 | tf_op jit(solution)/shard_map/while/body/eval_jaxpr/xcni,xcnj->xnij/dot_general | solution.py:50
  175.7 4.5 %fusion.237 = (f32[2,16,128]{2,1,0:T(8,128)S(1)}, f32[2,16,128]{2,1,0:T(8,128)S(1)}, f32[2,16,128,128]{2,3,1,0:T(8,128)S(1)}) fusion(f32[2,3,65,128]{3,1,2,0:T(4,128)S(1)} %get-tuple-element.447, s32[]{:T(128)S(6)} %select_n.174, f32[3]{0:T(128)S(1)} %get-tuple-element.453, s32[]{:T(128)S(6)} %select_n.173, ...), kind=kOutput, calls=%fused_computation.231.clone.1 | convolution fusion | flops 22548480 | bytes 2294280 | tf_op jit(solution)/shard_map/while/body/eval_jaxpr/xcni,xcnj->xnij/dot_general | solution.py:50
  191.6 4.5 %fusion.237 = (f32[2,16,128]{2,1,0:T(8,128)S(1)}, f32[2,16,128]{2,1,0:T(8,128)S(1)}, f32[2,16,128,128]{2,3,1,0:T(8,128)S(1)}) fusion(f32[2,3,65,128]{3,1,2,0:T(4,128)S(1)} %get-tuple-element.447, s32[]{:T(128)S(6)} %select_n.174, f32[3]{0:T(128)S(1)} %get-tuple-element.453, s32[]{:T(128)S(6)} %select_n.173, ...), kind=kOutput, calls=%fused_computation.231.clone.1 | convolution fusion | flops 22548480 | bytes 2294280 | tf_op jit(solution)/shard_map/while/body/eval_jaxpr/xcni,xcnj->xnij/dot_general | solution.py:50
  207.6 8.5 %copy.428 = f32[2,3,2,16,256]{1,2,0,4,3:T(2,128)} copy(f32[2,3,2,16,256]{4,2,1,0,3:T(2,128)S(1)} %bitcast.246) | data formatting | bytes 393216 | tf_op jit(solution)/shard_map/all_to_all | solution.py:156
  216.2 14.2 %reshape.169 = f32[16,1,3072]{2,1,0:T(1,128)} reshape(f32[4096,2,2,3]{3,2,1,0:T(2,128)} %bitcast.237) | data formatting | bytes 393216
  230.4 6.6 %all-to-all-start.3 = ((f32[16,1,3072]{2,1,0:T(1,128)}), f32[16,1,3072]{2,1,0:T(1,128)S(1)}, u32[]{:S(2)}, u32[]{:S(2)}) async-start(f32[16,1,3072]{2,1,0:T(1,128)} %reshape.169), calls=%async_computation.3 | async-start | bytes 393216 | tf_op jit(solution)/shard_map/all_to_all | solution.py:140
  237.3 8.3 %copy.384 = f32[2,3,2,4096]{1,2,0,3:T(2,128)} copy(f32[2,3,2,4096]{3,2,1,0:T(2,128)S(1)} %add_add_fusion) | data formatting | bytes 393216 | tf_op jit(solution)/shard_map/add | solution.py:136
  245.6 14.2 %reshape.171 = f32[16,1,3072]{2,1,0:T(1,128)} reshape(f32[4096,2,2,3]{3,2,1,0:T(2,128)} %bitcast.242) | data formatting | bytes 393216
  259.8 6.3 %all-to-all-start.5 = ((f32[16,1,3072]{2,1,0:T(1,128)}), f32[16,1,3072]{2,1,0:T(1,128)S(1)}, u32[]{:S(2)}, u32[]{:S(2)}) async-start(f32[16,1,3072]{2,1,0:T(1,128)} %reshape.171), calls=%async_computation.5 | async-start | bytes 393216 | tf_op jit(solution)/shard_map/all_to_all | solution.py:141
  269.3 14.8 %reshape.170 = f32[4096,2,2,3]{3,2,1,0:T(2,128)} reshape(f32[16,3072]{1,0:T(8,128)S(1)} %reduce.2) | data formatting | bytes 393216
  284.1 6.8 %copy.429 = f32[2,3,2,16,256]{4,3,2,1,0:T(8,128)S(1)} copy(f32[2,3,2,16,256]{1,2,0,4,3:T(2,128)} %bitcast.243) | data formatting | bytes 393216 | tf_op jit(solution)/shard_map/all_to_all | solution.py:140
  292.9 14.8 %reshape.172 = f32[4096,2,2,3]{3,2,1,0:T(2,128)} reshape(f32[16,3072]{1,0:T(8,128)S(1)} %reduce.3) | data formatting | bytes 393216
  307.7 7.3 %copy.433 = f32[2,3,2,16,256]{4,3,2,1,0:T(8,128)S(1)} copy(f32[2,3,2,16,256]{1,2,0,4,3:T(2,128)} %bitcast.244) | data formatting | bytes 393216 | tf_op jit(solution)/shard_map/all_to_all | solution.py:141
  320.4 6.3 %all-to-all-start.6 = ((f32[32,3,2,256]{3,2,1,0:T(2,128)}), f32[32,3,2,256]{3,2,1,0:T(2,128)S(1)}, u32[]{:S(2)}, u32[]{:S(2)}) async-start(f32[32,3,2,256]{3,2,1,0:T(2,128)} %copy.394), calls=%async_computation.6 | async-start | bytes 393216 | tf_op jit(solution)/shard_map/all_to_all | solution.py:156
  326.8 7.0 %all-to-all-done.6 = f32[32,3,2,256]{3,2,1,0:T(2,128)S(1)} async-done(((f32[32,3,2,256]{3,2,1,0:T(2,128)}), f32[32,3,2,256]{3,2,1,0:T(2,128)S(1)}, u32[]{:S(2)}, u32[]{:S(2)}) %all-to-all-start.6) | async-done | bytes 196640 | tf_op jit(solution)/shard_map/all_to_all | solution.py:156
  342.0 63.7 %while.33 = (s32[]{:T(128)}, f32[2,3,65,128]{3,1,2,0:T(4,128)S(1)}, f32[2,3,65,128]{3,1,2,0:T(4,128)S(1)}, s32[]{:T(128)}, s32[]{:T(128)}, /*index=5*/s32[]{:T(128)}, s32[]{:T(128)}, s32[]{:T(128)}, f32[3]{0:T(128)S(1)}) while((s32[]{:T(128)}, f32[2,3,65,128]{3,1,2,0:T(4,128)S(1)}, f32[2,3,65,128]{3,1,2,0:T(4,128)S(1)}, ...), condition=%wide.region_13.14_spmd.clone, body=%wide.region_7.13_spmd.sunk.clone.sunk | while | flops 101412872 | bytes 11750121 | solution.py:100
  358.2 4.5 %fusion.247 = (f32[2,16,128]{2,1,0:T(8,128)S(1)}, f32[2,16,128]{2,1,0:T(8,128)S(1)}, f32[2,16,128,128]{2,3,1,0:T(8,128)S(1)}) fusion(f32[2,3,65,128]{3,1,2,0:T(4,128)S(1)} %get-tuple-element.474, s32[]{:T(128)S(6)} %select_n.176, f32[3]{0:T(128)S(1)} %get-tuple-element.480, s32[]{:T(128)S(6)} %select_n.175, ...), kind=kOutput, calls=%fused_computation.232.clone.1 | convolution fusion | flops 22548480 | bytes 2294280 | tf_op jit(solution)/shard_map/while/body/eval_jaxpr/xcni,xcnj->xnij/dot_general | solution.py:50
  374.1 4.5 %fusion.247 = (f32[2,16,128]{2,1,0:T(8,128)S(1)}, f32[2,16,128]{2,1,0:T(8,128)S(1)}, f32[2,16,128,128]{2,3,1,0:T(8,128)S(1)}) fusion(f32[2,3,65,128]{3,1,2,0:T(4,128)S(1)} %get-tuple-element.474, s32[]{:T(128)S(6)} %select_n.176, f32[3]{0:T(128)S(1)} %get-tuple-element.480, s32[]{:T(128)S(6)} %select_n.175, ...), kind=kOutput, calls=%fused_computation.232.clone.1 | convolution fusion | flops 22548480 | bytes 2294280 | tf_op jit(solution)/shard_map/while/body/eval_jaxpr/xcni,xcnj->xnij/dot_general | solution.py:50
  (163 shorter events, 148.7 us)
Async XLA Ops:
  10.3 21.9 %copy-start.8 = (f32[32,5,5]{0,2,1:T(8,128)S(1)}, f32[32,5,5]{0,2,1:T(8,128)}, u32[]{:S(2)}) copy-start(f32[32,5,5]{0,2,1:T(8,128)} %param.16) | copy-start | bytes 9604
  10.3 22.0 %copy-start.9 = (f32[32,5,5]{0,2,1:T(8,128)S(1)}, f32[32,5,5]{0,2,1:T(8,128)}, u32[]{:S(2)}) copy-start(f32[32,5,5]{0,2,1:T(8,128)} %param.17) | copy-start | bytes 9604
  10.3 22.2 %copy-start.7 = (f32[2,3,8192]{2,0,1:T(2,128)S(1)}, f32[2,3,8192]{2,0,1:T(2,128)}, u32[]{:S(2)}) copy-start(f32[2,3,8192]{2,0,1:T(2,128)} %param.13) | copy-start | bytes 589828
  24.6 32.4 %all-to-all-start.1 = ((f32[16,1,3072]{2,1,0:T(1,128)}), f32[16,1,3072]{2,1,0:T(1,128)S(1)}, u32[]{:S(2)}, u32[]{:S(2)}) async-start(f32[16,1,3072]{2,1,0:T(1,128)} %reshape.167), calls=%async_computation.1 | async-start | bytes 393216 | tf_op jit(solution)/shard_map/all_to_all | solution.py:141
  57.0 34.1 %all-to-all-start = ((f32[16,1,3072]{2,1,0:T(1,128)}), f32[16,1,3072]{2,1,0:T(1,128)S(1)}, u32[]{:S(2)}, u32[]{:S(2)}) async-start(f32[16,1,3072]{2,1,0:T(1,128)} %reshape.165), calls=%async_computation | async-start | bytes 393216 | tf_op jit(solution)/shard_map/all_to_all | solution.py:140
  114.0 3.7 copy-start
  118.9 1.0 copy-start.1
  120.3 17.7 %copy-start.2 = (f32[32,5,3,512]{3,0,2,1:T(8,128)S(1)}, f32[32,5,3,512]{3,0,2,1:T(8,128)}, u32[]{:S(2)}) copy-start(f32[32,5,3,512]{3,0,2,1:T(8,128)} %copy-done.1) | copy-start | bytes 2949124
  121.2 13.4 %all-to-all-start.2 = ((f32[32,3,2,256]{3,2,1,0:T(2,128)}), f32[32,3,2,256]{3,2,1,0:T(2,128)S(1)}, u32[]{:S(2)}, u32[]{:S(2)}) async-start(f32[32,3,2,256]{3,2,1,0:T(2,128)} %copy.370), calls=%async_computation.2 | async-start | bytes 393216 | tf_op jit(solution)/shard_map/all_to_all | solution.py:156
  127.6 15.7 %copy-start.6 = (f32[3]{0:T(128)S(1)}, f32[3]{0:T(128)}, u32[]{:S(2)}) copy-start(f32[3]{0:T(128)} %constant.208.clone..sunk.4) | copy-start | bytes 40
  134.8 8.1 %collective-permute-start = (f32[2,3,128]{2,0,1:T(2,128)S(1)}, f32[2,3,128]{2,0,1:T(2,128)S(1)}, u32[]{:S(2)}, u32[]{:S(2)}) collective-permute-start(f32[2,3,128]{2,0,1:T(2,128)S(1)} %slice.57), channel_id=1, source_target_pairs={{1,0},{0,1},{3,2},{2,3},{5,4},{4,5},{7,6},{6,7},{9,8},{8,9},{11,10... | collective-permute-start | bytes 9224 | tf_op jit(solution)/shard_map/ppermute | solution.py:20
  139.4 76.8 %all-to-all-start.4 = ((f32[32,3,2,256]{3,2,1,0:T(2,128)}), f32[32,3,2,256]{3,2,1,0:T(2,128)S(1)}, u32[]{:S(2)}, u32[]{:S(2)}) async-start(f32[32,3,2,256]{3,2,1,0:T(2,128)} %copy.376), calls=%async_computation.4 | async-start | bytes 393216 | tf_op jit(solution)/shard_map/all_to_all | solution.py:159
  207.5 29.5 %collective-permute-start.1 = (f32[2,3,128]{2,1,0:T(4,128)S(1)}, f32[2,3,128]{2,1,0:T(4,128)S(1)}, u32[]{:S(2)}, u32[]{:S(2)}) collective-permute-start(f32[2,3,128]{2,1,0:T(4,128)S(1)} %slice_bitcast_fusion.9), channel_id=1, source_target_pairs={{1,0},{0,1},{3,2},{2,3},{5,4},{4,5},{7,6},{6,7},{9,8},{8,9},{11,10... | collective-permute-start | bytes 9224 | tf_op jit(solution)/shard_map/ppermute | solution.py:20
  230.4 29.4 %all-to-all-start.3 = ((f32[16,1,3072]{2,1,0:T(1,128)}), f32[16,1,3072]{2,1,0:T(1,128)S(1)}, u32[]{:S(2)}, u32[]{:S(2)}) async-start(f32[16,1,3072]{2,1,0:T(1,128)} %reshape.169), calls=%async_computation.3 | async-start | bytes 393216 | tf_op jit(solution)/shard_map/all_to_all | solution.py:140
  259.8 31.9 %all-to-all-start.5 = ((f32[16,1,3072]{2,1,0:T(1,128)}), f32[16,1,3072]{2,1,0:T(1,128)S(1)}, u32[]{:S(2)}, u32[]{:S(2)}) async-start(f32[16,1,3072]{2,1,0:T(1,128)} %reshape.171), calls=%async_computation.5 | async-start | bytes 393216 | tf_op jit(solution)/shard_map/all_to_all | solution.py:141
  307.7 8.2 %slice-start = ((f32[32,5,3,512]{3,0,2,1:T(8,128)}), f32[32,4,3,512]{3,0,2,1:T(8,128)S(1)}, s32[]{:S(2)}) async-start(f32[32,5,3,512]{3,0,2,1:T(8,128)} %copy-done.1), calls=%async_computation.8 | async-start | bytes 1572864 | tf_op jit(solution)/shard_map/slice | solution.py:119
  319.1 18.9 %copy-start.3 = (f32[32,5,3,512]{3,0,2,1:T(8,128)}, f32[32,5,3,512]{3,0,2,1:T(8,128)S(1)}, u32[]{:S(2)}) copy-start(f32[32,5,3,512]{3,0,2,1:T(8,128)S(1)} %bitcast_add_fusion) | copy-start | bytes 2949124
  320.4 13.4 %all-to-all-start.6 = ((f32[32,3,2,256]{3,2,1,0:T(2,128)}), f32[32,3,2,256]{3,2,1,0:T(2,128)S(1)}, u32[]{:S(2)}, u32[]{:S(2)}) async-start(f32[32,3,2,256]{3,2,1,0:T(2,128)} %copy.394), calls=%async_computation.6 | async-start | bytes 393216 | tf_op jit(solution)/shard_map/all_to_all | solution.py:156
  334.0 8.0 %copy-start.4 = (f32[2,3,8192]{2,0,1:T(2,128)}, f32[2,3,8192]{2,0,1:T(2,128)S(1)}, u32[]{:S(2)}) copy-start(f32[2,3,8192]{2,0,1:T(2,128)S(1)} %reshape.151) | copy-start | bytes 589828
  334.0 7.6 %collective-permute-start.2 = (f32[2,3,128]{2,0,1:T(2,128)S(1)}, f32[2,3,128]{2,0,1:T(2,128)S(1)}, u32[]{:S(2)}, u32[]{:S(2)}) collective-permute-start(f32[2,3,128]{2,0,1:T(2,128)S(1)} %slice.62), channel_id=1, source_target_pairs={{1,0},{0,1},{3,2},{2,3},{5,4},{4,5},{7,6},{6,7},{9,8},{8,9},{11,10... | collective-permute-start | bytes 9224 | tf_op jit(solution)/shard_map/ppermute | solution.py:20
  338.0 70.2 %all-to-all-start.7 = ((f32[32,3,2,256]{3,2,1,0:T(2,128)}), f32[32,3,2,256]{3,2,1,0:T(2,128)S(1)}, u32[]{:S(2)}, u32[]{:S(2)}) async-start(f32[32,3,2,256]{3,2,1,0:T(2,128)} %copy.396), calls=%async_computation.7 | async-start | bytes 393216 | tf_op jit(solution)/shard_map/all_to_all | solution.py:159
  405.7 1.1 slice-start.1
  405.7 2.8 collective-permute-start.3
  408.7 0.8 copy-start.5
where the time goes:
time: 416 us; the launch traced here: 410 us
  local copies, waits for them, and re-layouts  190 us (46%)
  matrix products  140 us (34%)
  starting transfers between devices  52.8 us (13%)
  waiting for transfers between devices  14 us (3%)
  other arithmetic  10.1 us (2%)
    unnamed x33, local copies, waits for them, and re-layouts  119 us
    dot_general x16, matrix products, tile_weight(): jnp.einsum('xcni,xcnj->xnij', center, other, precision=lax.Precision.HIGH...  68.3 us
    dot_general x8, matrix products, mutual(): jnp.einsum('xnij,xcni->xcnj', weight, center, precision=lax.Precision.HIG...  27.2 us
    dot_general x8, matrix products, pull(): jnp.einsum('xnij,xcnj->xcni', weight, other, precision=lax.Precision.HIGH...  15.2 us
    dot_general x8, matrix products, mutual(): jnp.einsum('xnij,xcnj->xcni', weight, other, precision=lax.Precision.HIGH...  15.2 us
    all_to_all x5, local copies, waits for them, and re-layouts, on_device(): lax.all_to_all(shaped_q, 'bead', split_axis=3, concat_axis=0, tiled=True)  14.7 us
    all_to_all x4, local copies, waits for them, and re-layouts, on_device(): lax.all_to_all(shaped_p, 'bead', split_axis=3, concat_axis=0, tiled=True)  14.4 us
    all_to_all x2, waiting for transfers between devices, on_device(): lax.all_to_all(new_q.reshape(BEADS, 3, 2, share), 'bead', split_axis=0, c...  14 us
  transfers between devices with their start and end apart: 12, of which 2 were waited for; matrix products, arithmetic and copies ran while one was open for 62% of the time, Pallas kernels for 0%

commit v1 on v0

--- a/solution.py
+++ b/solution.py
@@ -138,7 +138,15 @@
         shaped_p = momenta.reshape(beads_here, 3, 2, groups * share)
         owned_q, owned_p = (
             lax.all_to_all(shaped_q, "bead", split_axis=3, concat_axis=0, tiled=True),
-            lax.all_to_all(shaped_p, "bead", split_axis=3, concat_axis=0, tiled=True),
+            jnp.concatenate(
+                lax.all_to_all(
+                    jnp.stack(jnp.split(shaped_p, lax.psum(1, axis_name="bead"), axis=3)),
+                    concat_axis=0,
+                    axis_name="bead",
+                    split_axis=0,
+                ),
+                axis=0,
+            ),
         )
         new_q, new_p, aux = mode_step(
             owned_q.reshape(BEADS, 3, 2 * share),

time: 416 us -> 345 us (0.83)
  local copies, waits for them, and re-layouts: 190 us -> 122 us
    unnamed x33 -> x55, local copies, waits for them, and re-layouts: 119 us -> 80.6 us
    all_to_all x4 -> x2, local copies, waits for them, and re-layouts: 14.4 us -> 0.05 us  [on_device(): lax.all_to_all(jnp.stack(jnp.split(shaped_p, lax.psum(1, axis_name='bead'...]
    add x1 -> x0, local copies, waits for them, and re-layouts: 8.28 us -> none  [on_device(): momenta = momenta + half * force]
    reshape x2 -> x1, local copies, waits for them, and re-layouts: 8.52 us -> 0.24 us  [on_device(): shaped_p = momenta.reshape(beads_here, 3, 2, groups * share)]
  transfers between devices with their start and end apart: 12 -> 12, of which waited for: 2 -> 3; matrix products, arithmetic and copies ran while one was open for 62% -> 65% of each run, Pallas kernels for 0% -> 0%
where the time goes in v1:
time: 345 us; the launch traced here: 340 us
  matrix products  140 us (41%)
  local copies, waits for them, and re-layouts  122 us (35%)
  starting transfers between devices  50.4 us (15%)
  waiting for transfers between devices  16.9 us (5%)
  other arithmetic  7.94 us (2%)
    unnamed x55, local copies, waits for them, and re-layouts  80.6 us
    dot_general x16, matrix products, tile_weight(): jnp.einsum('xcni,xcnj->xnij', center, other, precision=lax.Precision.HIGH...  68.3 us
    dot_general x8, matrix products, mutual(): jnp.einsum('xnij,xcni->xcnj', weight, center, precision=lax.Precision.HIG...  27.2 us
    dot_general x8, matrix products, pull(): jnp.einsum('xnij,xcnj->xcni', weight, other, precision=lax.Precision.HIGH...  15.2 us
    dot_general x8, matrix products, mutual(): jnp.einsum('xnij,xcnj->xcni', weight, other, precision=lax.Precision.HIGH...  15.2 us
    all_to_all x5, local copies, waits for them, and re-layouts, on_device(): lax.all_to_all(shaped_q, 'bead', split_axis=3, concat_axis=0, tiled=True)  14.5 us
    all_to_all x2, waiting for transfers between devices, on_device(): lax.all_to_all(new_q.reshape(BEADS, 3, 2, share), 'bead', split_axis=0, c...  14 us
    all_to_all x2, starting transfers between devices, on_device(): lax.all_to_all(jnp.stack(jnp.split(shaped_p, lax.psum(1, axis_name='bead'...  13.7 us
  transfers between devices with their start and end apart: 12, of which 3 were waited for; matrix products, arithmetic and copies ran while one was open for 65% of the time, Pallas kernels for 0%

profile of v1, /device:TPU:1, one launch (start us, length us, event | category | flops | bytes accessed | tf_op | source)
XLA Modules:
  0.0 339.7 jit_solution(9942395685086071016)
XLA Ops:
  11.7 7.4 %all-to-all-start.1 = ((f32[16,2,3,2,256]{4,3,1,2,0:T(2,128)}), f32[16,2,3,2,256]{4,3,1,2,0:T(2,128)S(1)}, u32[]{:S(2)}, u32[]{:S(2)}) async-start(f32[16,2,3,2,256]{4,3,1,2,0:T(2,128)} %constant_dynamic-update-slice_fusion), calls=%async_computation.1 | async-start | bytes 393216 | tf_op jit(solution)/shard_map/all_to_all | solution.py:142
  21.2 8.3 %copy.398 = f32[2,3,2,4096]{1,2,0,3:T(2,128)} copy(f32[2,3,2,4096]{3,2,0,1:T(2,128)S(1)} %reshape.131) | data formatting | bytes 393216 | tf_op jit(solution)/shard_map/reshape | solution.py:137
  29.5 14.2 %reshape.155 = f32[16,1,3072]{2,1,0:T(1,128)} reshape(f32[4096,2,2,3]{3,2,1,0:T(2,128)} %bitcast.359) | data formatting | bytes 393216
  45.4 6.6 %all-to-all-start = ((f32[16,1,3072]{2,1,0:T(1,128)}), f32[16,1,3072]{2,1,0:T(1,128)S(1)}, u32[]{:S(2)}, u32[]{:S(2)}) async-start(f32[16,1,3072]{2,1,0:T(1,128)} %reshape.155), calls=%async_computation | async-start | bytes 393216 | tf_op jit(solution)/shard_map/all_to_all | solution.py:140
  60.6 14.8 %reshape.156 = f32[4096,2,2,3]{3,2,1,0:T(2,128)} reshape(f32[16,3072]{1,0:T(8,128)S(1)} %reduce) | data formatting | bytes 393216
  75.5 6.8 %copy.459 = f32[2,3,2,16,256]{4,3,2,1,0:T(8,128)S(1)} copy(f32[2,3,2,16,256]{1,2,0,4,3:T(2,128)} %bitcast.360) | data formatting | bytes 393216 | tf_op jit(solution)/shard_map/all_to_all | solution.py:140
  89.5 4.5 %all-to-all-start.2 = ((f32[32,3,2,256]{3,2,1,0:T(2,128)}), f32[32,3,2,256]{3,2,1,0:T(2,128)S(1)}, u32[]{:S(2)}, u32[]{:S(2)}) async-start(f32[32,3,2,256]{3,2,1,0:T(2,128)} %copy.410), calls=%async_computation.2 | async-start | bytes 393216 | tf_op jit(solution)/shard_map/all_to_all | solution.py:164
  94.1 6.9 %all-to-all-done.2 = f32[32,3,2,256]{3,2,1,0:T(2,128)S(1)} async-done(((f32[32,3,2,256]{3,2,1,0:T(2,128)}), f32[32,3,2,256]{3,2,1,0:T(2,128)S(1)}, u32[]{:S(2)}, u32[]{:S(2)}) %all-to-all-start.2) | async-done | bytes 196640 | tf_op jit(solution)/shard_map/all_to_all | solution.py:164
  109.2 64.1 %while.32 = (s32[]{:T(128)}, f32[2,3,65,128]{3,1,2,0:T(4,128)S(1)}, f32[2,3,65,128]{3,1,2,0:T(4,128)S(1)}, s32[]{:T(128)}, s32[]{:T(128)}, /*index=5*/s32[]{:T(128)}, s32[]{:T(128)}, s32[]{:T(128)}, f32[3]{0:T(128)S(1)}) while((s32[]{:T(128)}, f32[2,3,65,128]{3,1,2,0:T(4,128)S(1)}, f32[2,3,65,128]{3,1,2,0:T(4,128)S(1)}, ...), condition=%wide.region_6.7_spmd.clone, body=%wide.region_0.6_spmd.sunk.clone.sunk | while | flops 101412872 | bytes 11750121 | solution.py:100
  109.8 4.5 %fusion.237 = (f32[2,16,128]{2,1,0:T(8,128)S(1)}, f32[2,16,128]{2,1,0:T(8,128)S(1)}, f32[2,16,128,128]{2,3,1,0:T(8,128)S(1)}) fusion(f32[2,3,65,128]{3,1,2,0:T(4,128)S(1)} %get-tuple-element.445, s32[]{:T(128)S(6)} %select_n.174, f32[3]{0:T(128)S(1)} %get-tuple-element.451, s32[]{:T(128)S(6)} %select_n.173, ...), kind=kOutput, calls=%fused_computation.296.clone.1 | convolution fusion | flops 22548480 | bytes 2294280 | tf_op jit(solution)/shard_map/while/body/eval_jaxpr/xcni,xcnj->xnij/dot_general | solution.py:50
  116.3 4.0 %fusion.239 = (f32[2,16,128]{2,1,0:T(8,128)S(1)}, f32[2,16,128,128]{2,3,1,0:T(8,128)S(1)}) fusion(f32[2,3,65,128]{3,1,2,0:T(4,128)S(1)} %get-tuple-element.445, s32[]{:T(128)S(6)} %select_n.173, f32[2,16,128]{2,1,0:T(8,128)S(1)} %get-tuple-element.409), kind=kOutput, calls=%fused_computation.298.clone.1 | convolution fusion | flops 22016000 | bytes 2211844 | tf_op jit(solution)/shard_map/while/body/eval_jaxpr/xcni,xcnj->xnij/dot_general | solution.py:50
  125.7 4.5 %fusion.237 = (f32[2,16,128]{2,1,0:T(8,128)S(1)}, f32[2,16,128]{2,1,0:T(8,128)S(1)}, f32[2,16,128,128]{2,3,1,0:T(8,128)S(1)}) fusion(f32[2,3,65,128]{3,1,2,0:T(4,128)S(1)} %get-tuple-element.445, s32[]{:T(128)S(6)} %select_n.174, f32[3]{0:T(128)S(1)} %get-tuple-element.451, s32[]{:T(128)S(6)} %select_n.173, ...), kind=kOutput, calls=%fused_computation.296.clone.1 | convolution fusion | flops 22548480 | bytes 2294280 | tf_op jit(solution)/shard_map/while/body/eval_jaxpr/xcni,xcnj->xnij/dot_general | solution.py:50
  132.1 4.0 %fusion.239 = (f32[2,16,128]{2,1,0:T(8,128)S(1)}, f32[2,16,128,128]{2,3,1,0:T(8,128)S(1)}) fusion(f32[2,3,65,128]{3,1,2,0:T(4,128)S(1)} %get-tuple-element.445, s32[]{:T(128)S(6)} %select_n.173, f32[2,16,128]{2,1,0:T(8,128)S(1)} %get-tuple-element.409), kind=kOutput, calls=%fused_computation.298.clone.1 | convolution fusion | flops 22016000 | bytes 2211844 | tf_op jit(solution)/shard_map/while/body/eval_jaxpr/xcni,xcnj->xnij/dot_general | solution.py:50
  141.6 4.5 %fusion.237 = (f32[2,16,128]{2,1,0:T(8,128)S(1)}, f32[2,16,128]{2,1,0:T(8,128)S(1)}, f32[2,16,128,128]{2,3,1,0:T(8,128)S(1)}) fusion(f32[2,3,65,128]{3,1,2,0:T(4,128)S(1)} %get-tuple-element.445, s32[]{:T(128)S(6)} %select_n.174, f32[3]{0:T(128)S(1)} %get-tuple-element.451, s32[]{:T(128)S(6)} %select_n.173, ...), kind=kOutput, calls=%fused_computation.296.clone.1 | convolution fusion | flops 22548480 | bytes 2294280 | tf_op jit(solution)/shard_map/while/body/eval_jaxpr/xcni,xcnj->xnij/dot_general | solution.py:50
  148.0 4.0 %fusion.239 = (f32[2,16,128]{2,1,0:T(8,128)S(1)}, f32[2,16,128,128]{2,3,1,0:T(8,128)S(1)}) fusion(f32[2,3,65,128]{3,1,2,0:T(4,128)S(1)} %get-tuple-element.445, s32[]{:T(128)S(6)} %select_n.173, f32[2,16,128]{2,1,0:T(8,128)S(1)} %get-tuple-element.409), kind=kOutput, calls=%fused_computation.298.clone.1 | convolution fusion | flops 22016000 | bytes 2211844 | tf_op jit(solution)/shard_map/while/body/eval_jaxpr/xcni,xcnj->xnij/dot_general | solution.py:50
  157.5 4.5 %fusion.237 = (f32[2,16,128]{2,1,0:T(8,128)S(1)}, f32[2,16,128]{2,1,0:T(8,128)S(1)}, f32[2,16,128,128]{2,3,1,0:T(8,128)S(1)}) fusion(f32[2,3,65,128]{3,1,2,0:T(4,128)S(1)} %get-tuple-element.445, s32[]{:T(128)S(6)} %select_n.174, f32[3]{0:T(128)S(1)} %get-tuple-element.451, s32[]{:T(128)S(6)} %select_n.173, ...), kind=kOutput, calls=%fused_computation.296.clone.1 | convolution fusion | flops 22548480 | bytes 2294280 | tf_op jit(solution)/shard_map/while/body/eval_jaxpr/xcni,xcnj->xnij/dot_general | solution.py:50
  163.9 4.0 %fusion.239 = (f32[2,16,128]{2,1,0:T(8,128)S(1)}, f32[2,16,128,128]{2,3,1,0:T(8,128)S(1)}) fusion(f32[2,3,65,128]{3,1,2,0:T(4,128)S(1)} %get-tuple-element.445, s32[]{:T(128)S(6)} %select_n.173, f32[2,16,128]{2,1,0:T(8,128)S(1)} %get-tuple-element.409), kind=kOutput, calls=%fused_computation.298.clone.1 | convolution fusion | flops 22016000 | bytes 2211844 | tf_op jit(solution)/shard_map/while/body/eval_jaxpr/xcni,xcnj->xnij/dot_general | solution.py:50
  173.5 8.5 %copy.465 = f32[2,3,2,16,256]{1,2,0,4,3:T(2,128)} copy(f32[2,3,2,16,256]{4,2,1,0,3:T(2,128)S(1)} %bitcast.363) | data formatting | bytes 393216 | tf_op jit(solution)/shard_map/all_to_all | solution.py:164
  182.2 14.2 %reshape.157 = f32[16,1,3072]{2,1,0:T(1,128)} reshape(f32[4096,2,2,3]{3,2,1,0:T(2,128)} %bitcast.358) | data formatting | bytes 393216
  196.4 6.6 %all-to-all-start.3 = ((f32[16,1,3072]{2,1,0:T(1,128)}), f32[16,1,3072]{2,1,0:T(1,128)S(1)}, u32[]{:S(2)}, u32[]{:S(2)}) async-start(f32[16,1,3072]{2,1,0:T(1,128)} %reshape.157), calls=%async_computation.3 | async-start | bytes 393216 | tf_op jit(solution)/shard_map/all_to_all | solution.py:140
  213.0 6.3 %all-to-all-start.5 = ((f32[16,2,3,2,256]{4,3,2,1,0:T(2,128)}), f32[16,2,3,2,256]{4,3,2,1,0:T(2,128)S(1)}, u32[]{:S(2)}, u32[]{:S(2)}) async-start(f32[16,2,3,2,256]{4,3,2,1,0:T(2,128)} %constant_dynamic-update-slice_fusion.16), calls=%async_computation.5 | async-start | bytes 393216 | tf_op jit(solution)/shard_map/all_to_all | solution.py:142
  222.4 14.8 %reshape.158 = f32[4096,2,2,3]{3,2,1,0:T(2,128)} reshape(f32[16,3072]{1,0:T(8,128)S(1)} %reduce.1) | data formatting | bytes 393216
  237.2 6.8 %copy.466 = f32[2,3,2,16,256]{4,3,2,1,0:T(8,128)S(1)} copy(f32[2,3,2,16,256]{1,2,0,4,3:T(2,128)} %bitcast.361) | data formatting | bytes 393216 | tf_op jit(solution)/shard_map/all_to_all | solution.py:140
  250.2 6.3 %all-to-all-start.6 = ((f32[32,3,2,256]{3,2,1,0:T(2,128)}), f32[32,3,2,256]{3,2,1,0:T(2,128)S(1)}, u32[]{:S(2)}, u32[]{:S(2)}) async-start(f32[32,3,2,256]{3,2,1,0:T(2,128)} %copy.432), calls=%async_computation.6 | async-start | bytes 393216 | tf_op jit(solution)/shard_map/all_to_all | solution.py:164
  256.6 7.0 %all-to-all-done.6 = f32[32,3,2,256]{3,2,1,0:T(2,128)S(1)} async-done(((f32[32,3,2,256]{3,2,1,0:T(2,128)}), f32[32,3,2,256]{3,2,1,0:T(2,128)S(1)}, u32[]{:S(2)}, u32[]{:S(2)}) %all-to-all-start.6) | async-done | bytes 196640 | tf_op jit(solution)/shard_map/all_to_all | solution.py:164
  271.8 63.7 %while.33 = (s32[]{:T(128)}, f32[2,3,65,128]{3,1,2,0:T(4,128)S(1)}, f32[2,3,65,128]{3,1,2,0:T(4,128)S(1)}, s32[]{:T(128)}, s32[]{:T(128)}, /*index=5*/s32[]{:T(128)}, s32[]{:T(128)}, s32[]{:T(128)}, f32[3]{0:T(128)S(1)}) while((s32[]{:T(128)}, f32[2,3,65,128]{3,1,2,0:T(4,128)S(1)}, f32[2,3,65,128]{3,1,2,0:T(4,128)S(1)}, ...), condition=%wide.region_13.14_spmd.clone, body=%wide.region_7.13_spmd.sunk.clone.sunk | while | flops 101412872 | bytes 11750121 | solution.py:100
  272.2 4.5 %fusion.247 = (f32[2,16,128]{2,1,0:T(8,128)S(1)}, f32[2,16,128]{2,1,0:T(8,128)S(1)}, f32[2,16,128,128]{2,3,1,0:T(8,128)S(1)}) fusion(f32[2,3,65,128]{3,1,2,0:T(4,128)S(1)} %get-tuple-element.472, s32[]{:T(128)S(6)} %select_n.176, f32[3]{0:T(128)S(1)} %get-tuple-element.478, s32[]{:T(128)S(6)} %select_n.175, ...), kind=kOutput, calls=%fused_computation.297.clone.1 | convolution fusion | flops 22548480 | bytes 2294280 | tf_op jit(solution)/shard_map/while/body/eval_jaxpr/xcni,xcnj->xnij/dot_general | solution.py:50
  278.6 4.0 %fusion.249 = (f32[2,16,128]{2,1,0:T(8,128)S(1)}, f32[2,16,128,128]{2,3,1,0:T(8,128)S(1)}) fusion(f32[2,3,65,128]{3,1,2,0:T(4,128)S(1)} %get-tuple-element.472, s32[]{:T(128)S(6)} %select_n.175, f32[2,16,128]{2,1,0:T(8,128)S(1)} %get-tuple-element.419), kind=kOutput, calls=%fused_computation.299.clone.1 | convolution fusion | flops 22016000 | bytes 2211844 | tf_op jit(solution)/shard_map/while/body/eval_jaxpr/xcni,xcnj->xnij/dot_general | solution.py:50
  288.1 4.5 %fusion.247 = (f32[2,16,128]{2,1,0:T(8,128)S(1)}, f32[2,16,128]{2,1,0:T(8,128)S(1)}, f32[2,16,128,128]{2,3,1,0:T(8,128)S(1)}) fusion(f32[2,3,65,128]{3,1,2,0:T(4,128)S(1)} %get-tuple-element.472, s32[]{:T(128)S(6)} %select_n.176, f32[3]{0:T(128)S(1)} %get-tuple-element.478, s32[]{:T(128)S(6)} %select_n.175, ...), kind=kOutput, calls=%fused_computation.297.clone.1 | convolution fusion | flops 22548480 | bytes 2294280 | tf_op jit(solution)/shard_map/while/body/eval_jaxpr/xcni,xcnj->xnij/dot_general | solution.py:50
  294.5 4.0 %fusion.249 = (f32[2,16,128]{2,1,0:T(8,128)S(1)}, f32[2,16,128,128]{2,3,1,0:T(8,128)S(1)}) fusion(f32[2,3,65,128]{3,1,2,0:T(4,128)S(1)} %get-tuple-element.472, s32[]{:T(128)S(6)} %select_n.175, f32[2,16,128]{2,1,0:T(8,128)S(1)} %get-tuple-element.419), kind=kOutput, calls=%fused_computation.299.clone.1 | convolution fusion | flops 22016000 | bytes 2211844 | tf_op jit(solution)/shard_map/while/body/eval_jaxpr/xcni,xcnj->xnij/dot_general | solution.py:50
  303.9 4.5 %fusion.247 = (f32[2,16,128]{2,1,0:T(8,128)S(1)}, f32[2,16,128]{2,1,0:T(8,128)S(1)}, f32[2,16,128,128]{2,3,1,0:T(8,128)S(1)}) fusion(f32[2,3,65,128]{3,1,2,0:T(4,128)S(1)} %get-tuple-element.472, s32[]{:T(128)S(6)} %select_n.176, f32[3]{0:T(128)S(1)} %get-tuple-element.478, s32[]{:T(128)S(6)} %select_n.175, ...), kind=kOutput, calls=%fused_computation.297.clone.1 | convolution fusion | flops 22548480 | bytes 2294280 | tf_op jit(solution)/shard_map/while/body/eval_jaxpr/xcni,xcnj->xnij/dot_general | solution.py:50
  319.8 4.5 %fusion.247 = (f32[2,16,128]{2,1,0:T(8,128)S(1)}, f32[2,16,128]{2,1,0:T(8,128)S(1)}, f32[2,16,128,128]{2,3,1,0:T(8,128)S(1)}) fusion(f32[2,3,65,128]{3,1,2,0:T(4,128)S(1)} %get-tuple-element.472, s32[]{:T(128)S(6)} %select_n.176, f32[3]{0:T(128)S(1)} %get-tuple-element.478, s32[]{:T(128)S(6)} %select_n.175, ...), kind=kOutput, calls=%fused_computation.297.clone.1 | convolution fusion | flops 22548480 | bytes 2294280 | tf_op jit(solution)/shard_map/while/body/eval_jaxpr/xcni,xcnj->xnij/dot_general | solution.py:50
  (183 shorter events, 136.3 us)
Async XLA Ops:
  0.6 20.4 %copy-start.7 = (f32[2,3,8192]{2,0,1:T(2,128)S(1)}, f32[2,3,8192]{2,0,1:T(2,128)}, u32[]{:S(2)}) copy-start(f32[2,3,8192]{2,0,1:T(2,128)} %param.13) | copy-start | bytes 589828
  11.7 33.7 %all-to-all-start.1 = ((f32[16,2,3,2,256]{4,3,1,2,0:T(2,128)}), f32[16,2,3,2,256]{4,3,1,2,0:T(2,128)S(1)}, u32[]{:S(2)}, u32[]{:S(2)}) async-start(f32[16,2,3,2,256]{4,3,1,2,0:T(2,128)} %constant_dynamic-update-slice_fusion), calls=%async_computation.1 | async-start | bytes 393216 | tf_op jit(solution)/shard_map/all_to_all | solution.py:142
  45.4 13.6 %all-to-all-start = ((f32[16,1,3072]{2,1,0:T(1,128)}), f32[16,1,3072]{2,1,0:T(1,128)S(1)}, u32[]{:S(2)}, u32[]{:S(2)}) async-start(f32[16,1,3072]{2,1,0:T(1,128)} %reshape.155), calls=%async_computation | async-start | bytes 393216 | tf_op jit(solution)/shard_map/all_to_all | solution.py:140
  82.3 3.7 %copy-start = (f32[32,5,3,512]{3,1,2,0:T(8,128)S(1)}, f32[32,5,3,512]{3,1,2,0:T(8,128)}, u32[]{:S(2)}) copy-start(f32[32,5,3,512]{3,1,2,0:T(8,128)} %fusion.43) | copy-start | bytes 2949124
  87.2 1.0 copy-start.1
  88.6 15.3 %copy-start.2 = (f32[32,5,3,512]{3,0,2,1:T(8,128)S(1)}, f32[32,5,3,512]{3,0,2,1:T(8,128)}, u32[]{:S(2)}) copy-start(f32[32,5,3,512]{3,0,2,1:T(8,128)} %copy-done.1) | copy-start | bytes 2949124
  89.5 11.5 %all-to-all-start.2 = ((f32[32,3,2,256]{3,2,1,0:T(2,128)}), f32[32,3,2,256]{3,2,1,0:T(2,128)S(1)}, u32[]{:S(2)}, u32[]{:S(2)}) async-start(f32[32,3,2,256]{3,2,1,0:T(2,128)} %copy.410), calls=%async_computation.2 | async-start | bytes 393216 | tf_op jit(solution)/shard_map/all_to_all | solution.py:164
  94.0 15.2 %copy-start.6 = (f32[3]{0:T(128)S(1)}, f32[3]{0:T(128)}, u32[]{:S(2)}) copy-start(f32[3]{0:T(128)} %constant.208.clone..sunk.4) | copy-start | bytes 40
  101.2 7.6 %collective-permute-start = (f32[2,3,128]{2,0,1:T(2,128)S(1)}, f32[2,3,128]{2,0,1:T(2,128)S(1)}, u32[]{:S(2)}, u32[]{:S(2)}) collective-permute-start(f32[2,3,128]{2,0,1:T(2,128)S(1)} %slice.57), channel_id=1, source_target_pairs={{1,0},{0,1},{3,2},{2,3},{5,4},{4,5},{7,6},{6,7},{9,8},{8,9},{11,10... | collective-permute-start | bytes 9224 | tf_op jit(solution)/shard_map/ppermute | solution.py:20
  105.2 76.7 %all-to-all-start.4 = ((f32[32,3,2,256]{3,2,1,0:T(2,128)}), f32[32,3,2,256]{3,2,1,0:T(2,128)S(1)}, u32[]{:S(2)}, u32[]{:S(2)}) async-start(f32[32,3,2,256]{3,2,1,0:T(2,128)} %copy.416), calls=%async_computation.4 | async-start | bytes 393216 | tf_op jit(solution)/shard_map/all_to_all | solution.py:167
  173.4 29.6 %collective-permute-start.1 = (f32[2,3,128]{2,1,0:T(4,128)S(1)}, f32[2,3,128]{2,1,0:T(4,128)S(1)}, u32[]{:S(2)}, u32[]{:S(2)}) collective-permute-start(f32[2,3,128]{2,1,0:T(4,128)S(1)} %slice_bitcast_fusion.41), channel_id=1, source_target_pairs={{1,0},{0,1},{3,2},{2,3},{5,4},{4,5},{7,6},{6,7},{9,8},{8,9},{11,10... | collective-permute-start | bytes 9224 | tf_op jit(solution)/shard_map/ppermute | solution.py:20
  196.4 16.6 %all-to-all-start.3 = ((f32[16,1,3072]{2,1,0:T(1,128)}), f32[16,1,3072]{2,1,0:T(1,128)S(1)}, u32[]{:S(2)}, u32[]{:S(2)}) async-start(f32[16,1,3072]{2,1,0:T(1,128)} %reshape.157), calls=%async_computation.3 | async-start | bytes 393216 | tf_op jit(solution)/shard_map/all_to_all | solution.py:140
  213.0 32.0 %all-to-all-start.5 = ((f32[16,2,3,2,256]{4,3,2,1,0:T(2,128)}), f32[16,2,3,2,256]{4,3,2,1,0:T(2,128)S(1)}, u32[]{:S(2)}, u32[]{:S(2)}) async-start(f32[16,2,3,2,256]{4,3,2,1,0:T(2,128)} %constant_dynamic-update-slice_fusion.16), calls=%async_computation.5 | async-start | bytes 393216 | tf_op jit(solution)/shard_map/all_to_all | solution.py:142
  244.1 1.6 slice-start
  248.9 18.9 %copy-start.3 = (f32[32,5,3,512]{3,0,2,1:T(8,128)}, f32[32,5,3,512]{3,0,2,1:T(8,128)S(1)}, u32[]{:S(2)}) copy-start(f32[32,5,3,512]{3,0,2,1:T(8,128)S(1)} %bitcast_add_fusion) | copy-start | bytes 2949124
  250.2 13.4 %all-to-all-start.6 = ((f32[32,3,2,256]{3,2,1,0:T(2,128)}), f32[32,3,2,256]{3,2,1,0:T(2,128)S(1)}, u32[]{:S(2)}, u32[]{:S(2)}) async-start(f32[32,3,2,256]{3,2,1,0:T(2,128)} %copy.432), calls=%async_computation.6 | async-start | bytes 393216 | tf_op jit(solution)/shard_map/all_to_all | solution.py:164
  263.8 8.0 %copy-start.4 = (f32[2,3,8192]{2,0,1:T(2,128)}, f32[2,3,8192]{2,0,1:T(2,128)S(1)}, u32[]{:S(2)}) copy-start(f32[2,3,8192]{2,0,1:T(2,128)S(1)} %reshape.141) | copy-start | bytes 589828
  263.8 7.5 %collective-permute-start.2 = (f32[2,3,128]{2,0,1:T(2,128)S(1)}, f32[2,3,128]{2,0,1:T(2,128)S(1)}, u32[]{:S(2)}, u32[]{:S(2)}) collective-permute-start(f32[2,3,128]{2,0,1:T(2,128)S(1)} %slice.62), channel_id=1, source_target_pairs={{1,0},{0,1},{3,2},{2,3},{5,4},{4,5},{7,6},{6,7},{9,8},{8,9},{11,10... | collective-permute-start | bytes 9224 | tf_op jit(solution)/shard_map/ppermute | solution.py:20
  267.9 70.2 %all-to-all-start.7 = ((f32[32,3,2,256]{3,2,1,0:T(2,128)}), f32[32,3,2,256]{3,2,1,0:T(2,128)S(1)}, u32[]{:S(2)}, u32[]{:S(2)}) async-start(f32[32,3,2,256]{3,2,1,0:T(2,128)} %copy.434), calls=%async_computation.7 | async-start | bytes 393216 | tf_op jit(solution)/shard_map/all_to_all | solution.py:167
  335.5 1.1 slice-start.1
  335.6 2.8 collective-permute-start.3
  338.5 0.8 copy-start.5
